TPU v7x, 32 devices: a whole 2x2x4 slice. The times are simulated.
32 devices in a mesh: dp: 8 (over y, x, core), mp: 4 (over z).
Axes of the slice: x: 2, y: 2, z: 4, core: 2. Of those that a mesh axis runs over, the one named last changes fastest.
Arguments:
- buffer: bfloat16 [65536, 256], P(('dp', 'mp')), may hold values from -24 to 24, as said below
- owner: int32 [32768, 1], P(('dp', 'mp')), may hold values from 0 to 31; in each aligned block of 1024 rows (0 to 1023, 1024 to 2047, ...) at most 128 rows name the same one
- local_row: int32 [32768], P(('dp', 'mp')), may hold values from 0 to 2047
- q_in: bfloat16 [2, 130, 256], replicated, may hold values from -0.5 to 0.5
- q_mid: bfloat16 [2, 256, 256], replicated, may hold values from -0.5 to 0.5
- q_out: bfloat16 [2, 256], replicated, may hold values from -0.5 to 0.5
- v_in: bfloat16 [124, 256], replicated, may hold values from -0.5 to 0.5
- v_mid: bfloat16 [256, 256], replicated, may hold values from -0.5 to 0.5
- v_out: bfloat16 [256], replicated, may hold values from -0.5 to 0.5
Outputs:
- q_values: float32 [2, 32768], P(None, ('dp', 'mp'))
- values: float32 [2, 32768], P(None, ('dp', 'mp'))
- targets: float32 [32768], P(('dp', 'mp'))
- q_loss: float32 [32768], P(('dp', 'mp'))
- value_loss: float32 [32768], P(('dp', 'mp'))
Inputs may be any that keep to these rules, and one draw needn't show every extreme that they name: Owner o is the replay owner at position o of the devices in dp+mp order. In the rows of one reader no owner is named more than 128 times, a bound that some block reaches. `buffer`: action values lie in -1 to 1 and discounts in 0 to 0.99.
All inputs are finite; a program needn't handle non-finite values.
Results may differ from a plain program's by a relative error of at most 0.005.
Values may be sent and summed in bfloat16 or wider, within the bound.
A program may use at most 64 MiB of HBM per device.

v0:
```python
import jax
import jax.numpy as jnp
from jax import lax
from jax.sharding import PartitionSpec as P


def layer_two(first, mid, out):
    hidden = jnp.maximum(jnp.dot(first, mid, preferred_element_type=jnp.float32), 0.0)
    return jnp.dot(hidden, out.astype(jnp.float32), precision=lax.Precision.HIGHEST)


def critic_block(rows, weights, states_width, pair_width):
    q_in, q_mid, q_out, v_in, v_mid, v_out = weights
    pair = rows[:, :pair_width]
    state = rows[:, :states_width]
    nexts = rows[:, pair_width : pair_width + states_width]
    reward = rows[:, pair_width + states_width].astype(jnp.float32)
    discount = rows[:, pair_width + states_width + 1].astype(jnp.float32)
    first_one = jnp.maximum(jnp.dot(pair, q_in[0], preferred_element_type=jnp.float32), 0.0).astype(
        jnp.bfloat16
    )
    first_two = jnp.maximum(jnp.dot(pair, q_in[1], preferred_element_type=jnp.float32), 0.0).astype(
        jnp.bfloat16
    )
    q_first = layer_two(first_one, q_mid[0], q_out[0])
    q_second = layer_two(first_two, q_mid[1], q_out[1])
    both = jnp.concatenate([state, nexts], axis=0)
    first_value = jnp.maximum(jnp.dot(both, v_in, preferred_element_type=jnp.float32), 0.0).astype(
        jnp.bfloat16
    )
    value_all = layer_two(first_value, v_mid, v_out)
    count = state.shape[0]
    value_now = value_all[:count]
    value_next = value_all[count:]
    targets = reward + discount * value_next
    return (q_first, q_second, value_now, value_next, targets)


def body(buffer, owner, local_row, q_in, q_mid, q_out, v_in, v_mid, v_out):
    outer = lax.axis_size("dp")
    inner = lax.axis_size("mp")
    owners = outer * inner
    batch = local_row.shape[0]
    columns_all = buffer.shape[1]
    states_width = v_in.shape[0]
    pair_width = q_in.shape[1]
    weights = (q_in, q_mid, q_out, v_in, v_mid, v_out)
    slots_each = max(2, 4 * batch // owners)
    target_owner = owner[:, 0]
    positions = jnp.arange(batch, dtype=jnp.int32)
    same_owner = target_owner[:, None] == target_owner[None, :]
    earlier = positions[None, :] < positions[:, None]
    placed = jnp.sum(jnp.logical_and(same_owner, earlier).astype(jnp.int32), axis=1)
    owner_hot = (target_owner[:, None] == jnp.arange(owners, dtype=jnp.int32)[None, :]).astype(
        jnp.float32
    )
    place_hot = (placed[:, None] == jnp.arange(slots_each, dtype=jnp.int32)[None, :]).astype(
        jnp.float32
    )
    weighted = place_hot * (local_row.astype(jnp.float32) + 1.0)[:, None]
    table = jnp.dot(owner_hot.T, weighted, precision=lax.Precision.HIGHEST)
    requests = (table.astype(jnp.int32) - 1).reshape(outer, inner, slots_each)
    asked = lax.all_to_all(
        lax.all_to_all(requests, "dp", split_axis=0, concat_axis=0, tiled=True),
        "mp",
        split_axis=1,
        concat_axis=1,
        tiled=True,
    )
    picked = jnp.take(buffer, jnp.maximum(asked, 0).reshape(-1), axis=0)

    def evaluate(block):
        return jnp.stack(critic_block(block, weights, states_width, pair_width))

    served = lax.map(evaluate, picked.reshape(outer, inner * slots_each, columns_all))
    served = served.reshape(outer, 5, inner, slots_each)
    returned = lax.all_to_all(
        lax.all_to_all(served, "dp", split_axis=0, concat_axis=0, tiled=True),
        "mp",
        split_axis=2,
        concat_axis=2,
        tiled=True,
    )
    flat = jnp.transpose(returned, (1, 0, 2, 3)).reshape(5, owners, slots_each)
    by_slot = jnp.einsum("kos,bs->kob", flat, place_hot, precision=lax.Precision.HIGHEST)
    mine = jnp.einsum("kob,bo->kb", by_slot, owner_hot, precision=lax.Precision.HIGHEST)
    q_first, q_second, value_now, value_next, targets = (
        mine[0],
        mine[1],
        mine[2],
        mine[3],
        mine[4],
    )
    q_loss = (q_first - targets) ** 2 + (q_second - targets) ** 2
    gap = jnp.minimum(q_first, q_second) - value_now
    value_loss = jnp.where(gap < 0.0, 0.3, 0.7) * gap * gap
    return (
        jnp.stack([q_first, q_second]),
        jnp.stack([value_now, value_next]),
        targets,
        q_loss,
        value_loss,
    )


def solution(mesh):
    return jax.shard_map(
        body,
        mesh=mesh,
        in_specs=(
            P(("dp", "mp"), None),
            P(("dp", "mp"), None),
            P(("dp", "mp")),
            P(),
            P(),
            P(),
            P(),
            P(),
            P(),
        ),
        out_specs=(
            P(None, ("dp", "mp")),
            P(None, ("dp", "mp")),
            P(("dp", "mp")),
            P(("dp", "mp")),
            P(("dp", "mp")),
        ),
        check_vma=False,
    )
```

profile of v0, /device:TPU:0, one launch (start us, length us, event | category | flops | bytes accessed | tf_op | source)
XLA Modules:
  0.0 118.4 jit_solution(8527828568259253387)
XLA Ops:
  2.7 1.7 %fusion.42 = s32[32,128]{1,0:T(8,128)S(1)} fusion(f32[1024]{0:T(1024)S(1)} %convert_add_fusion, s32[1024]{0:T(1024)S(1)} %convert_reduce_fusion, s32[1024]{0:T(1024)} %bitcast.126), kind=kOutput, calls=%fused_computation.48 | convolution fusion | flops 50634752 | bytes 28672 | tf_op jit(solution)/shard_map/dot_general | solution.py:61
  4.4 9.8 %all_to_all.20 = s32[8,4,128]{2,1,0:T(4,128)S(1)} all-to-all(s32[8,4,128]{2,1,0:T(4,128)S(1)} %bitcast.119), channel_id=1, replica_groups=mesh['dp'=8,'mp'=4] {'dp'}, dimensions={0} | all-to-all | bytes 32768 | tf_op jit(solution)/shard_map/all_to_all | solution.py:64
  14.8 4.9 %all-to-all-start.1 = ((s32[8,4,128]{2,0,1:T(8,128)}), s32[8,4,128]{2,0,1:T(8,128)S(1)}, u32[]{:S(2)}, u32[]{:S(2)}) async-start(s32[8,4,128]{2,0,1:T(8,128)} %copy.41), calls=%async_computation.1 | async-start | bytes 32768 | tf_op jit(solution)/shard_map/all_to_all | solution.py:63
  20.6 4.7 %all-to-all-done.1 = s32[8,4,128]{2,0,1:T(8,128)S(1)} async-done(((s32[8,4,128]{2,0,1:T(8,128)}), s32[8,4,128]{2,0,1:T(8,128)S(1)}, u32[]{:S(2)}, u32[]{:S(2)}) %all-to-all-start.1) | async-done | bytes 16416 | tf_op jit(solution)/shard_map/all_to_all | solution.py:63
  25.3 16.9 %gather_fusion = bf16[4096,256]{1,0:T(8,128)(2,1)} fusion(bf16[2048,256]{1,0:T(8,128)(2,1)S(1)} %copy-done, s32[4096]{0:T(1024)S(1)} %broadcast_clamp_fusion), kind=kCustom, calls=%fused_computation | custom fusion | bytes 4210688 | tf_op jit(solution)/shard_map/jit(_take)/gather | solution.py:70
  42.3 2.9 %copy.43 = bf16[8,512,256]{1,2,0:T(8,128)(2,1)S(1)} copy(bf16[8,512,256]{2,1,0:T(8,128)(2,1)} %bitcast.104) | data formatting | bytes 4194304 | tf_op jit(solution)/shard_map/jit(_take)/gather | solution.py:70
  45.2 1.5 %broadcast_select_fusion = bf16[8,512,256]{1,2,0:T(8,128)(2,1)} fusion(bf16[8,512,256]{1,2,0:T(8,128)(2,1)S(1)} %copy.43, pred[8,512]{1,0:T(8,128)(4,1)S(1)} %compare_and_fusion), kind=kLoop, calls=%fused_computation.43 | loop fusion | flops 1048576 | bytes 4198400 | tf_op jit(solution)/shard_map/jit(_take)/select_n | solution.py:70
  46.7 51.7 %while.10 = (s32[]{:T(128)}, f32[8,5,512]{2,0,1:T(8,128)}, bf16[8,512,256]{1,2,0:T(8,128)(2,1)}, bf16[2,130,256]{2,1,0:T(8,128)(2,1)S(1)}, bf16[2,256,256]{2,1,0...) while((s32[]{:T(128)}, f32[8,5,512]{2,0,1:T(8,128)}, ...), condition=%wide.region_2.3_spmd, body=%wide.region_1.2_spmd.sunk | while | flops 409978880 | bytes 7499437 | solution.py:75
  47.8 1.5 %convolution_maximum_fusion.11 = f32[1024,256]{1,0:T(8,128)S(1)} fusion(bf16[256,256]{1,0:T(8,128)(2,1)} %get-tuple-element.229, bf16[124,256]{1,0:T(8,128)(2,1)} %get-tuple-element.228, bf16[512,124]{0,1:T(8,128)(2,1)S(1)} %get-tuple-element.195, bf16[512,124]{0,1:T(8,128)(2,1)S(1)} %get-tuple-element.196), kind=kOutput, calls=%fused_computation.1.clone.1 | convolution fusion | flops 200523776 | bytes 1497088 | tf_op jit(solution)/shard_map/while/body/eval_jaxpr/dot_general | solution.py:8
  51.6 1.6 %dynamic_update_slice.5 = f32[8,5,512]{2,0,1:T(8,128)} dynamic-update-slice(f32[8,5,512]{2,0,1:T(8,128)} %get-tuple-element.212, f32[1,5,512]{2,0,1:T(1,128)S(1)} %copy.60, s32[]{:T(128)} %get-tuple-element.211, s32[]{:T(128)} %constant.20.clone.1..sunk, s32[]{:T(128)} %constant.20.clone.1..sunk) | dynamic-update-slice | bytes 20484 | tf_op jit(solution)/shard_map/while/body/jit(dynamic_update_index_in_dim)/dynamic_update_slice | solution.py:75
  58.1 1.6 %dynamic_update_slice.5 = f32[8,5,512]{2,0,1:T(8,128)} dynamic-update-slice(f32[8,5,512]{2,0,1:T(8,128)} %get-tuple-element.212, f32[1,5,512]{2,0,1:T(1,128)S(1)} %copy.60, s32[]{:T(128)} %get-tuple-element.211, s32[]{:T(128)} %constant.20.clone.1..sunk, s32[]{:T(128)} %constant.20.clone.1..sunk) | dynamic-update-slice | bytes 20484 | tf_op jit(solution)/shard_map/while/body/jit(dynamic_update_index_in_dim)/dynamic_update_slice | solution.py:75
  60.7 1.5 %convolution_maximum_fusion.11 = f32[1024,256]{1,0:T(8,128)S(1)} fusion(bf16[256,256]{1,0:T(8,128)(2,1)} %get-tuple-element.229, bf16[124,256]{1,0:T(8,128)(2,1)} %get-tuple-element.228, bf16[512,124]{0,1:T(8,128)(2,1)S(1)} %get-tuple-element.195, bf16[512,124]{0,1:T(8,128)(2,1)S(1)} %get-tuple-element.196), kind=kOutput, calls=%fused_computation.1.clone.1 | convolution fusion | flops 200523776 | bytes 1497088 | tf_op jit(solution)/shard_map/while/body/eval_jaxpr/dot_general | solution.py:8
  64.5 1.6 %dynamic_update_slice.5 = f32[8,5,512]{2,0,1:T(8,128)} dynamic-update-slice(f32[8,5,512]{2,0,1:T(8,128)} %get-tuple-element.212, f32[1,5,512]{2,0,1:T(1,128)S(1)} %copy.60, s32[]{:T(128)} %get-tuple-element.211, s32[]{:T(128)} %constant.20.clone.1..sunk, s32[]{:T(128)} %constant.20.clone.1..sunk) | dynamic-update-slice | bytes 20484 | tf_op jit(solution)/shard_map/while/body/jit(dynamic_update_index_in_dim)/dynamic_update_slice | solution.py:75
  71.0 1.6 %dynamic_update_slice.5 = f32[8,5,512]{2,0,1:T(8,128)} dynamic-update-slice(f32[8,5,512]{2,0,1:T(8,128)} %get-tuple-element.212, f32[1,5,512]{2,0,1:T(1,128)S(1)} %copy.60, s32[]{:T(128)} %get-tuple-element.211, s32[]{:T(128)} %constant.20.clone.1..sunk, s32[]{:T(128)} %constant.20.clone.1..sunk) | dynamic-update-slice | bytes 20484 | tf_op jit(solution)/shard_map/while/body/jit(dynamic_update_index_in_dim)/dynamic_update_slice | solution.py:75
  73.6 1.5 %convolution_maximum_fusion.11 = f32[1024,256]{1,0:T(8,128)S(1)} fusion(bf16[256,256]{1,0:T(8,128)(2,1)} %get-tuple-element.229, bf16[124,256]{1,0:T(8,128)(2,1)} %get-tuple-element.228, bf16[512,124]{0,1:T(8,128)(2,1)S(1)} %get-tuple-element.195, bf16[512,124]{0,1:T(8,128)(2,1)S(1)} %get-tuple-element.196), kind=kOutput, calls=%fused_computation.1.clone.1 | convolution fusion | flops 200523776 | bytes 1497088 | tf_op jit(solution)/shard_map/while/body/eval_jaxpr/dot_general | solution.py:8
  77.5 1.6 %dynamic_update_slice.5 = f32[8,5,512]{2,0,1:T(8,128)} dynamic-update-slice(f32[8,5,512]{2,0,1:T(8,128)} %get-tuple-element.212, f32[1,5,512]{2,0,1:T(1,128)S(1)} %copy.60, s32[]{:T(128)} %get-tuple-element.211, s32[]{:T(128)} %constant.20.clone.1..sunk, s32[]{:T(128)} %constant.20.clone.1..sunk) | dynamic-update-slice | bytes 20484 | tf_op jit(solution)/shard_map/while/body/jit(dynamic_update_index_in_dim)/dynamic_update_slice | solution.py:75
  80.1 1.5 %convolution_maximum_fusion.11 = f32[1024,256]{1,0:T(8,128)S(1)} fusion(bf16[256,256]{1,0:T(8,128)(2,1)} %get-tuple-element.229, bf16[124,256]{1,0:T(8,128)(2,1)} %get-tuple-element.228, bf16[512,124]{0,1:T(8,128)(2,1)S(1)} %get-tuple-element.195, bf16[512,124]{0,1:T(8,128)(2,1)S(1)} %get-tuple-element.196), kind=kOutput, calls=%fused_computation.1.clone.1 | convolution fusion | flops 200523776 | bytes 1497088 | tf_op jit(solution)/shard_map/while/body/eval_jaxpr/dot_general | solution.py:8
  83.9 1.6 %dynamic_update_slice.5 = f32[8,5,512]{2,0,1:T(8,128)} dynamic-update-slice(f32[8,5,512]{2,0,1:T(8,128)} %get-tuple-element.212, f32[1,5,512]{2,0,1:T(1,128)S(1)} %copy.60, s32[]{:T(128)} %get-tuple-element.211, s32[]{:T(128)} %constant.20.clone.1..sunk, s32[]{:T(128)} %constant.20.clone.1..sunk) | dynamic-update-slice | bytes 20484 | tf_op jit(solution)/shard_map/while/body/jit(dynamic_update_index_in_dim)/dynamic_update_slice | solution.py:75
  86.5 1.5 %convolution_maximum_fusion.11 = f32[1024,256]{1,0:T(8,128)S(1)} fusion(bf16[256,256]{1,0:T(8,128)(2,1)} %get-tuple-element.229, bf16[124,256]{1,0:T(8,128)(2,1)} %get-tuple-element.228, bf16[512,124]{0,1:T(8,128)(2,1)S(1)} %get-tuple-element.195, bf16[512,124]{0,1:T(8,128)(2,1)S(1)} %get-tuple-element.196), kind=kOutput, calls=%fused_computation.1.clone.1 | convolution fusion | flops 200523776 | bytes 1497088 | tf_op jit(solution)/shard_map/while/body/eval_jaxpr/dot_general | solution.py:8
  90.4 1.6 %dynamic_update_slice.5 = f32[8,5,512]{2,0,1:T(8,128)} dynamic-update-slice(f32[8,5,512]{2,0,1:T(8,128)} %get-tuple-element.212, f32[1,5,512]{2,0,1:T(1,128)S(1)} %copy.60, s32[]{:T(128)} %get-tuple-element.211, s32[]{:T(128)} %constant.20.clone.1..sunk, s32[]{:T(128)} %constant.20.clone.1..sunk) | dynamic-update-slice | bytes 20484 | tf_op jit(solution)/shard_map/while/body/jit(dynamic_update_index_in_dim)/dynamic_update_slice | solution.py:75
  96.8 1.6 %dynamic_update_slice.5 = f32[8,5,512]{2,0,1:T(8,128)} dynamic-update-slice(f32[8,5,512]{2,0,1:T(8,128)} %get-tuple-element.212, f32[1,5,512]{2,0,1:T(1,128)S(1)} %copy.60, s32[]{:T(128)} %get-tuple-element.211, s32[]{:T(128)} %constant.20.clone.1..sunk, s32[]{:T(128)} %constant.20.clone.1..sunk) | dynamic-update-slice | bytes 20484 | tf_op jit(solution)/shard_map/while/body/jit(dynamic_update_index_in_dim)/dynamic_update_slice | solution.py:75
  99.3 7.5 %all_to_all.21 = f32[8,5,4,128]{3,2,1,0:T(4,128)S(1)} all-to-all(f32[8,5,4,128]{3,2,1,0:T(4,128)S(1)} %copy.46), channel_id=1, replica_groups=mesh['dp'=8,'mp'=4] {'dp'}, dimensions={0} | all-to-all | bytes 163840 | tf_op jit(solution)/shard_map/all_to_all | solution.py:78
  107.4 3.3 %all-to-all-start.3 = ((f32[8,5,4,128]{3,0,1,2:T(8,128)}), f32[8,5,4,128]{3,0,1,2:T(8,128)S(1)}, u32[]{:S(2)}, u32[]{:S(2)}) async-start(f32[8,5,4,128]{3,0,1,2:T(8,128)} %copy.47), calls=%async_computation.3 | async-start | bytes 163840 | tf_op jit(solution)/shard_map/all_to_all | solution.py:77
  111.1 5.4 %all-to-all-done.3 = f32[8,5,4,128]{3,0,1,2:T(8,128)S(1)} async-done(((f32[8,5,4,128]{3,0,1,2:T(8,128)}), f32[8,5,4,128]{3,0,1,2:T(8,128)S(1)}, u32[]{:S(2)}, u32[]{:S(2)}) %all-to-all-start.3) | async-done | bytes 81952 | tf_op jit(solution)/shard_map/all_to_all | solution.py:77
  (162 shorter events, 38.4 us)
Async XLA Ops:
  0.6 24.7 %copy-start = (bf16[2048,256]{1,0:T(8,128)(2,1)S(1)}, bf16[2048,256]{1,0:T(8,128)(2,1)}, u32[]{:S(2)}) copy-start(bf16[2048,256]{1,0:T(8,128)(2,1)} %param.11) | copy-start | bytes 3145732
  2.0 2.4 %copy-start.6 = (s32[1024]{0:T(1024)}, s32[1024]{0:T(1024)S(1)}, u32[]{:S(2)}) copy-start(s32[1024]{0:T(1024)S(1)} %convert_reduce_fusion) | copy-start | bytes 12292
  14.8 10.5 %all-to-all-start.1 = ((s32[8,4,128]{2,0,1:T(8,128)}), s32[8,4,128]{2,0,1:T(8,128)S(1)}, u32[]{:S(2)}, u32[]{:S(2)}) async-start(s32[8,4,128]{2,0,1:T(8,128)} %copy.41), calls=%async_computation.1 | async-start | bytes 32768 | tf_op jit(solution)/shard_map/all_to_all | solution.py:63
  45.1 1.5 %copy-start.1 = (bf16[2,256]{1,0:T(2,128)(2,1)S(1)}, bf16[2,256]{1,0:T(2,128)(2,1)}, u32[]{:S(2)}) copy-start(bf16[2,256]{1,0:T(2,128)(2,1)} %param.16) | copy-start | bytes 3076
  46.7 64.0 %copy-start.3 = (s32[1024,1]{0,1:T(1,128)S(1)}, s32[1024,1]{0,1:T(1,128)}, u32[]{:S(2)}) copy-start(s32[1024,1]{0,1:T(1,128)} %param.12) | copy-start | bytes 12292
  46.7 69.8 %copy-start.7 = (s32[1024]{0:T(1024)S(1)}, s32[1024]{0:T(1024)}, u32[]{:S(2)}) copy-start(s32[1024]{0:T(1024)} %copy-done.6) | copy-start | bytes 12292
  46.7 2.6 %copy-start.5 = (bf16[256]{0:T(256)(128)(2,1)S(1)}, bf16[256]{0:T(256)(128)(2,1)}, u32[]{:S(2)}) copy-start(bf16[256]{0:T(256)(128)(2,1)} %get-tuple-element.230) | copy-start | bytes 1540 | tf_op jit(solution)/shard_map/while
  46.7 3.2 %copy-start.4 = (bf16[2,256,256]{2,1,0:T(8,128)(2,1)S(1)}, bf16[2,256,256]{2,1,0:T(8,128)(2,1)}, u32[]{:S(2)}) copy-start(bf16[2,256,256]{2,1,0:T(8,128)(2,1)} %get-tuple-element.226) | copy-start | bytes 786436 | tf_op jit(solution)/shard_map/while
  53.2 2.6 %copy-start.5 = (bf16[256]{0:T(256)(128)(2,1)S(1)}, bf16[256]{0:T(256)(128)(2,1)}, u32[]{:S(2)}) copy-start(bf16[256]{0:T(256)(128)(2,1)} %get-tuple-element.230) | copy-start | bytes 1540 | tf_op jit(solution)/shard_map/while
  53.2 3.2 %copy-start.4 = (bf16[2,256,256]{2,1,0:T(8,128)(2,1)S(1)}, bf16[2,256,256]{2,1,0:T(8,128)(2,1)}, u32[]{:S(2)}) copy-start(bf16[2,256,256]{2,1,0:T(8,128)(2,1)} %get-tuple-element.226) | copy-start | bytes 786436 | tf_op jit(solution)/shard_map/while
  59.6 2.6 %copy-start.5 = (bf16[256]{0:T(256)(128)(2,1)S(1)}, bf16[256]{0:T(256)(128)(2,1)}, u32[]{:S(2)}) copy-start(bf16[256]{0:T(256)(128)(2,1)} %get-tuple-element.230) | copy-start | bytes 1540 | tf_op jit(solution)/shard_map/while
  59.6 3.2 %copy-start.4 = (bf16[2,256,256]{2,1,0:T(8,128)(2,1)S(1)}, bf16[2,256,256]{2,1,0:T(8,128)(2,1)}, u32[]{:S(2)}) copy-start(bf16[2,256,256]{2,1,0:T(8,128)(2,1)} %get-tuple-element.226) | copy-start | bytes 786436 | tf_op jit(solution)/shard_map/while
  66.1 2.6 %copy-start.5 = (bf16[256]{0:T(256)(128)(2,1)S(1)}, bf16[256]{0:T(256)(128)(2,1)}, u32[]{:S(2)}) copy-start(bf16[256]{0:T(256)(128)(2,1)} %get-tuple-element.230) | copy-start | bytes 1540 | tf_op jit(solution)/shard_map/while
  66.1 3.2 %copy-start.4 = (bf16[2,256,256]{2,1,0:T(8,128)(2,1)S(1)}, bf16[2,256,256]{2,1,0:T(8,128)(2,1)}, u32[]{:S(2)}) copy-start(bf16[2,256,256]{2,1,0:T(8,128)(2,1)} %get-tuple-element.226) | copy-start | bytes 786436 | tf_op jit(solution)/shard_map/while
  72.6 2.6 %copy-start.5 = (bf16[256]{0:T(256)(128)(2,1)S(1)}, bf16[256]{0:T(256)(128)(2,1)}, u32[]{:S(2)}) copy-start(bf16[256]{0:T(256)(128)(2,1)} %get-tuple-element.230) | copy-start | bytes 1540 | tf_op jit(solution)/shard_map/while
  72.6 3.2 %copy-start.4 = (bf16[2,256,256]{2,1,0:T(8,128)(2,1)S(1)}, bf16[2,256,256]{2,1,0:T(8,128)(2,1)}, u32[]{:S(2)}) copy-start(bf16[2,256,256]{2,1,0:T(8,128)(2,1)} %get-tuple-element.226) | copy-start | bytes 786436 | tf_op jit(solution)/shard_map/while
  79.0 2.6 %copy-start.5 = (bf16[256]{0:T(256)(128)(2,1)S(1)}, bf16[256]{0:T(256)(128)(2,1)}, u32[]{:S(2)}) copy-start(bf16[256]{0:T(256)(128)(2,1)} %get-tuple-element.230) | copy-start | bytes 1540 | tf_op jit(solution)/shard_map/while
  79.0 3.2 %copy-start.4 = (bf16[2,256,256]{2,1,0:T(8,128)(2,1)S(1)}, bf16[2,256,256]{2,1,0:T(8,128)(2,1)}, u32[]{:S(2)}) copy-start(bf16[2,256,256]{2,1,0:T(8,128)(2,1)} %get-tuple-element.226) | copy-start | bytes 786436 | tf_op jit(solution)/shard_map/while
  85.5 2.6 %copy-start.5 = (bf16[256]{0:T(256)(128)(2,1)S(1)}, bf16[256]{0:T(256)(128)(2,1)}, u32[]{:S(2)}) copy-start(bf16[256]{0:T(256)(128)(2,1)} %get-tuple-element.230) | copy-start | bytes 1540 | tf_op jit(solution)/shard_map/while
  85.5 3.2 %copy-start.4 = (bf16[2,256,256]{2,1,0:T(8,128)(2,1)S(1)}, bf16[2,256,256]{2,1,0:T(8,128)(2,1)}, u32[]{:S(2)}) copy-start(bf16[2,256,256]{2,1,0:T(8,128)(2,1)} %get-tuple-element.226) | copy-start | bytes 786436 | tf_op jit(solution)/shard_map/while
  91.9 2.6 %copy-start.5 = (bf16[256]{0:T(256)(128)(2,1)S(1)}, bf16[256]{0:T(256)(128)(2,1)}, u32[]{:S(2)}) copy-start(bf16[256]{0:T(256)(128)(2,1)} %get-tuple-element.230) | copy-start | bytes 1540 | tf_op jit(solution)/shard_map/while
  91.9 3.2 %copy-start.4 = (bf16[2,256,256]{2,1,0:T(8,128)(2,1)S(1)}, bf16[2,256,256]{2,1,0:T(8,128)(2,1)}, u32[]{:S(2)}) copy-start(bf16[2,256,256]{2,1,0:T(8,128)(2,1)} %get-tuple-element.226) | copy-start | bytes 786436 | tf_op jit(solution)/shard_map/while
  107.4 9.1 %all-to-all-start.3 = ((f32[8,5,4,128]{3,0,1,2:T(8,128)}), f32[8,5,4,128]{3,0,1,2:T(8,128)S(1)}, u32[]{:S(2)}, u32[]{:S(2)}) async-start(f32[8,5,4,128]{3,0,1,2:T(8,128)} %copy.47), calls=%async_computation.3 | async-start | bytes 163840 | tf_op jit(solution)/shard_map/all_to_all | solution.py:77
  117.1 1.2 %copy-start.2 = (f32[1,1024]{1,0:T(1,128)}, f32[1,1024]{1,0:T(1,128)S(1)}, u32[]{:S(2)}) copy-start(f32[1,1024]{1,0:T(1,128)S(1)} %get-tuple-element.126) | copy-start | bytes 12292
where the time goes:
time: 120 us; the launch traced here: 118 us
  local copies, waits for them, and re-layouts  45.1 us (38%)
  matrix products  31.9 us (27%)
  blocking collectives  17.2 us (14%)
  waiting for transfers between devices  10.1 us (8%)
  starting transfers between devices  8.16 us (7%)
  other arithmetic  4.53 us (4%)
    gather x2, local copies, waits for them, and re-layouts, body(): picked = jnp.take(buffer, jnp.maximum(asked, 0).reshape(-1), axis=0)  19.8 us
    dot_general x24, matrix products, layer_two(): jnp.dot(first, mid, preferred_element_type=jnp.float32)  19.4 us
    dynamic_update_slice x16, local copies, waits for them, and re-layouts, body(): lax.map(evaluate, picked.reshape(outer, inner * slots_each, columns_all))  12.5 us
    dot_general x24, matrix products, layer_two(): jnp.dot(hidden, out.astype(jnp.float32), precision=lax.Precision.HIGHEST)  10.2 us
    all_to_all x1, blocking collectives, body(): lax.all_to_all(requests, 'dp', split_axis=0, concat_axis=0, tiled=True)  9.75 us
    squeeze x8, local copies, waits for them, and re-layouts, body(): lax.map(evaluate, picked.reshape(outer, inner * slots_each, columns_all))  8.09 us
    all_to_all x1, blocking collectives, body(): lax.all_to_all(served, 'dp', split_axis=0, concat_axis=0, tiled=True)  7.49 us
    all_to_all x1, waiting for transfers between devices, body(): lax.all_to_all(lax.all_to_all(served, 'dp', split_axis=0, concat_axis=0,...  5.37 us
  transfers between devices with their start and end apart: 2, of which 2 were waited for; matrix products, arithmetic and copies ran while one was open for 1% of the time, Pallas kernels for 0%

commit v1 on v0

--- a/solution.py
+++ b/solution.py
@@ -60,12 +60,20 @@
     weighted = place_hot * (local_row.astype(jnp.float32) + 1.0)[:, None]
     table = jnp.dot(owner_hot.T, weighted, precision=lax.Precision.HIGHEST)
     requests = (table.astype(jnp.int32) - 1).reshape(outer, inner, slots_each)
-    asked = lax.all_to_all(
-        lax.all_to_all(requests, "dp", split_axis=0, concat_axis=0, tiled=True),
-        "mp",
-        split_axis=1,
-        concat_axis=1,
-        tiled=True,
+    asked = jnp.concatenate(
+        lax.all_to_all(
+            jnp.stack(
+                jnp.split(
+                    lax.all_to_all(requests, "dp", split_axis=0, concat_axis=0, tiled=True),
+                    lax.axis_size("mp"),
+                    axis=1,
+                )
+            ),
+            "mp",
+            0,
+            0,
+        ),
+        axis=1,
     )
     picked = jnp.take(buffer, jnp.maximum(asked, 0).reshape(-1), axis=0)
 

time: 120 us -> 106 us (0.88)
  local copies, waits for them, and re-layouts: 45.1 us -> 31.9 us
    dynamic_update_slice x16, local copies, waits for them, and re-layouts: 12.5 us -> 0.79 us  [body(): lax.map(evaluate, picked.reshape(outer, inner * slots_each, columns_all))]
where the time goes in v1:
time: 106 us; the launch traced here: 105 us
  local copies, waits for them, and re-layouts  31.9 us (30%)
  matrix products  31 us (29%)
  blocking collectives  17.2 us (16%)
  waiting for transfers between devices  10.1 us (10%)
  starting transfers between devices  8.16 us (8%)
  other arithmetic  5.12 us (5%)
    gather x2, local copies, waits for them, and re-layouts, body(): picked = jnp.take(buffer, jnp.maximum(asked, 0).reshape(-1), axis=0)  19.8 us
    dot_general x24, matrix products, layer_two(): jnp.dot(first, mid, preferred_element_type=jnp.float32)  18.5 us
    dot_general x24, matrix products, layer_two(): jnp.dot(hidden, out.astype(jnp.float32), precision=lax.Precision.HIGHEST)  10.2 us
    all_to_all x1, blocking collectives, body(): lax.all_to_all(requests, 'dp', split_axis=0, concat_axis=0, tiled=True)  9.75 us
    squeeze x8, local copies, waits for them, and re-layouts, body(): lax.map(evaluate, picked.reshape(outer, inner * slots_each, columns_all))  8.12 us
    all_to_all x1, blocking collectives, body(): lax.all_to_all(served, 'dp', split_axis=0, concat_axis=0, tiled=True)  7.49 us
    all_to_all x1, waiting for transfers between devices, body(): lax.all_to_all(lax.all_to_all(served, 'dp', split_axis=0, concat_axis=0,...  5.37 us
    all_to_all x1, starting transfers between devices, body(): lax.all_to_all(jnp.stack(jnp.split(lax.all_to_all(requests, 'dp', split_a...  4.87 us
  transfers between devices with their start and end apart: 2, of which 2 were waited for; matrix products, arithmetic and copies ran while one was open for 1% of the time, Pallas kernels for 0%

profile of v1, /device:TPU:0, one launch (start us, length us, event | category | flops | bytes accessed | tf_op | source)
XLA Modules:
  0.0 105.1 jit_solution(4600635458612219945)
XLA Ops:
  0.6 1.3 %convert_reduce_fusion = s32[1024]{0:T(1024)S(1)} fusion(s32[1024]{0:T(1024)} %bitcast.139), kind=kLoop, calls=%fused_computation.40 | loop fusion | flops 5241856 | bytes 8192 | tf_op jit(solution)/shard_map/reduce_sum | solution.py:53
  2.6 1.7 %fusion.42 = s32[32,128]{1,0:T(8,128)S(1)} fusion(f32[1024]{0:T(1024)S(1)} %convert_add_fusion, s32[1024]{0:T(1024)S(1)} %convert_reduce_fusion, s32[1024]{0:T(1024)} %bitcast.140), kind=kOutput, calls=%fused_computation.48 | convolution fusion | flops 50634752 | bytes 28672 | tf_op jit(solution)/shard_map/dot_general | solution.py:61
  4.4 9.8 %all_to_all.20 = s32[8,4,128]{2,1,0:T(4,128)S(1)} all-to-all(s32[8,4,128]{2,1,0:T(4,128)S(1)} %bitcast.129), channel_id=1, replica_groups=mesh['dp'=8,'mp'=4] {'dp'}, dimensions={0} | all-to-all | bytes 32768 | tf_op jit(solution)/shard_map/all_to_all | solution.py:67
  14.8 4.9 %all-to-all-start.1 = ((s32[4,8,1,128]{3,1,2,0:T(8,128)}), s32[4,8,1,128]{3,1,2,0:T(8,128)S(1)}, u32[]{:S(2)}, u32[]{:S(2)}) async-start(s32[4,8,1,128]{3,1,2,0:T(8,128)} %pad_add_fusion), calls=%async_computation.1 | async-start | bytes 32768 | tf_op jit(solution)/shard_map/all_to_all | solution.py:64
  20.6 4.7 %all-to-all-done.1 = s32[4,8,1,128]{3,1,2,0:T(8,128)S(1)} async-done(((s32[4,8,1,128]{3,1,2,0:T(8,128)}), s32[4,8,1,128]{3,1,2,0:T(8,128)S(1)}, u32[]{:S(2)}, u32[]{:S(2)}) %all-to-all-start.1) | async-done | bytes 16416 | tf_op jit(solution)/shard_map/all_to_all | solution.py:64
  25.3 16.9 %gather_fusion = bf16[4096,256]{1,0:T(8,128)(2,1)} fusion(bf16[2048,256]{1,0:T(8,128)(2,1)S(1)} %copy-done, s32[4096]{0:T(1024)S(1)} %broadcast_clamp_fusion), kind=kCustom, calls=%fused_computation | custom fusion | bytes 4210688 | tf_op jit(solution)/shard_map/jit(_take)/gather | solution.py:78
  42.2 2.9 %copy.39 = bf16[8,512,256]{1,2,0:T(8,128)(2,1)S(1)} copy(bf16[8,512,256]{2,1,0:T(8,128)(2,1)} %bitcast.115) | data formatting | bytes 4194304 | tf_op jit(solution)/shard_map/jit(_take)/gather | solution.py:78
  45.1 1.5 %broadcast_select_fusion = bf16[8,512,256]{1,2,0:T(8,128)(2,1)} fusion(bf16[8,512,256]{1,2,0:T(8,128)(2,1)S(1)} %copy.39, pred[8,512]{1,0:T(8,128)(4,1)S(1)} %compare_bitcast_fusion), kind=kLoop, calls=%fused_computation.43 | loop fusion | flops 1048576 | bytes 4198400 | tf_op jit(solution)/shard_map/jit(_take)/select_n | solution.py:78
  46.7 39.3 %while.10 = (s32[]{:T(128)}, f32[8,5,512]{2,0,1:T(8,128)S(1)}, bf16[8,512,256]{1,2,0:T(8,128)(2,1)}, bf16[2,130,256]{2,1,0:T(8,128)(2,1)S(1)}, bf16[2,256,256]{2...) while((s32[]{:T(128)}, f32[8,5,512]{2,0,1:T(8,128)S(1)}, ...), condition=%wide.region_2.3_spmd, body=%wide.region_1.2_spmd.sunk | while | flops 409978880 | bytes 7497361 | solution.py:83
  46.7 1.0 dynamic-slice_bitcast_fusion.2
  47.8 1.4 %convolution_maximum_fusion.11 = f32[1024,256]{1,0:T(8,128)S(1)} fusion(bf16[256,256]{1,0:T(8,128)(2,1)S(1)} %get-tuple-element.215, bf16[124,256]{1,0:T(8,128)(2,1)} %get-tuple-element.214, bf16[512,124]{0,1:T(8,128)(2,1)S(1)} %get-tuple-element.181, bf16[512,124]{0,1:T(8,128)(2,1)S(1)} %get-tuple-element.182), kind=kOutput, calls=%fused_computation.1.clone.1 | convolution fusion | flops 200523776 | bytes 1497088 | tf_op jit(solution)/shard_map/while/body/eval_jaxpr/dot_general | solution.py:8
  51.6 1.0 dynamic-slice_bitcast_fusion.2
  52.7 1.4 %convolution_maximum_fusion.11 = f32[1024,256]{1,0:T(8,128)S(1)} fusion(bf16[256,256]{1,0:T(8,128)(2,1)S(1)} %get-tuple-element.215, bf16[124,256]{1,0:T(8,128)(2,1)} %get-tuple-element.214, bf16[512,124]{0,1:T(8,128)(2,1)S(1)} %get-tuple-element.181, bf16[512,124]{0,1:T(8,128)(2,1)S(1)} %get-tuple-element.182), kind=kOutput, calls=%fused_computation.1.clone.1 | convolution fusion | flops 200523776 | bytes 1497088 | tf_op jit(solution)/shard_map/while/body/eval_jaxpr/dot_general | solution.py:8
  56.5 1.0 dynamic-slice_bitcast_fusion.2
  57.6 1.4 %convolution_maximum_fusion.11 = f32[1024,256]{1,0:T(8,128)S(1)} fusion(bf16[256,256]{1,0:T(8,128)(2,1)S(1)} %get-tuple-element.215, bf16[124,256]{1,0:T(8,128)(2,1)} %get-tuple-element.214, bf16[512,124]{0,1:T(8,128)(2,1)S(1)} %get-tuple-element.181, bf16[512,124]{0,1:T(8,128)(2,1)S(1)} %get-tuple-element.182), kind=kOutput, calls=%fused_computation.1.clone.1 | convolution fusion | flops 200523776 | bytes 1497088 | tf_op jit(solution)/shard_map/while/body/eval_jaxpr/dot_general | solution.py:8
  61.5 1.0 dynamic-slice_bitcast_fusion.2
  62.5 1.4 %convolution_maximum_fusion.11 = f32[1024,256]{1,0:T(8,128)S(1)} fusion(bf16[256,256]{1,0:T(8,128)(2,1)S(1)} %get-tuple-element.215, bf16[124,256]{1,0:T(8,128)(2,1)} %get-tuple-element.214, bf16[512,124]{0,1:T(8,128)(2,1)S(1)} %get-tuple-element.181, bf16[512,124]{0,1:T(8,128)(2,1)S(1)} %get-tuple-element.182), kind=kOutput, calls=%fused_computation.1.clone.1 | convolution fusion | flops 200523776 | bytes 1497088 | tf_op jit(solution)/shard_map/while/body/eval_jaxpr/dot_general | solution.py:8
  67.4 1.4 %convolution_maximum_fusion.11 = f32[1024,256]{1,0:T(8,128)S(1)} fusion(bf16[256,256]{1,0:T(8,128)(2,1)S(1)} %get-tuple-element.215, bf16[124,256]{1,0:T(8,128)(2,1)} %get-tuple-element.214, bf16[512,124]{0,1:T(8,128)(2,1)S(1)} %get-tuple-element.181, bf16[512,124]{0,1:T(8,128)(2,1)S(1)} %get-tuple-element.182), kind=kOutput, calls=%fused_computation.1.clone.1 | convolution fusion | flops 200523776 | bytes 1497088 | tf_op jit(solution)/shard_map/while/body/eval_jaxpr/dot_general | solution.py:8
  72.3 1.4 %convolution_maximum_fusion.11 = f32[1024,256]{1,0:T(8,128)S(1)} fusion(bf16[256,256]{1,0:T(8,128)(2,1)S(1)} %get-tuple-element.215, bf16[124,256]{1,0:T(8,128)(2,1)} %get-tuple-element.214, bf16[512,124]{0,1:T(8,128)(2,1)S(1)} %get-tuple-element.181, bf16[512,124]{0,1:T(8,128)(2,1)S(1)} %get-tuple-element.182), kind=kOutput, calls=%fused_computation.1.clone.1 | convolution fusion | flops 200523776 | bytes 1497088 | tf_op jit(solution)/shard_map/while/body/eval_jaxpr/dot_general | solution.py:8
  77.2 1.4 %convolution_maximum_fusion.11 = f32[1024,256]{1,0:T(8,128)S(1)} fusion(bf16[256,256]{1,0:T(8,128)(2,1)S(1)} %get-tuple-element.215, bf16[124,256]{1,0:T(8,128)(2,1)} %get-tuple-element.214, bf16[512,124]{0,1:T(8,128)(2,1)S(1)} %get-tuple-element.181, bf16[512,124]{0,1:T(8,128)(2,1)S(1)} %get-tuple-element.182), kind=kOutput, calls=%fused_computation.1.clone.1 | convolution fusion | flops 200523776 | bytes 1497088 | tf_op jit(solution)/shard_map/while/body/eval_jaxpr/dot_general | solution.py:8
  82.2 1.4 %convolution_maximum_fusion.11 = f32[1024,256]{1,0:T(8,128)S(1)} fusion(bf16[256,256]{1,0:T(8,128)(2,1)S(1)} %get-tuple-element.215, bf16[124,256]{1,0:T(8,128)(2,1)} %get-tuple-element.214, bf16[512,124]{0,1:T(8,128)(2,1)S(1)} %get-tuple-element.181, bf16[512,124]{0,1:T(8,128)(2,1)S(1)} %get-tuple-element.182), kind=kOutput, calls=%fused_computation.1.clone.1 | convolution fusion | flops 200523776 | bytes 1497088 | tf_op jit(solution)/shard_map/while/body/eval_jaxpr/dot_general | solution.py:8
  86.0 7.5 %all_to_all.21 = f32[8,5,4,128]{3,2,1,0:T(4,128)S(1)} all-to-all(f32[8,5,4,128]{3,2,1,0:T(4,128)S(1)} %copy.42), channel_id=1, replica_groups=mesh['dp'=8,'mp'=4] {'dp'}, dimensions={0} | all-to-all | bytes 163840 | tf_op jit(solution)/shard_map/all_to_all | solution.py:86
  94.1 3.3 %all-to-all-start.3 = ((f32[8,5,4,128]{3,0,1,2:T(8,128)}), f32[8,5,4,128]{3,0,1,2:T(8,128)S(1)}, u32[]{:S(2)}, u32[]{:S(2)}) async-start(f32[8,5,4,128]{3,0,1,2:T(8,128)} %copy.43), calls=%async_computation.3 | async-start | bytes 163840 | tf_op jit(solution)/shard_map/all_to_all | solution.py:85
  97.8 5.4 %all-to-all-done.3 = f32[8,5,4,128]{3,0,1,2:T(8,128)S(1)} async-done(((f32[8,5,4,128]{3,0,1,2:T(8,128)}), f32[8,5,4,128]{3,0,1,2:T(8,128)S(1)}, u32[]{:S(2)}, u32[]{:S(2)}) %all-to-all-start.3) | async-done | bytes 81952 | tf_op jit(solution)/shard_map/all_to_all | solution.py:85
  (146 shorter events, 28.4 us)
Async XLA Ops:
  0.6 24.6 %copy-start = (bf16[2048,256]{1,0:T(8,128)(2,1)S(1)}, bf16[2048,256]{1,0:T(8,128)(2,1)}, u32[]{:S(2)}) copy-start(bf16[2048,256]{1,0:T(8,128)(2,1)} %param.11) | copy-start | bytes 3145732
  14.8 10.5 %all-to-all-start.1 = ((s32[4,8,1,128]{3,1,2,0:T(8,128)}), s32[4,8,1,128]{3,1,2,0:T(8,128)S(1)}, u32[]{:S(2)}, u32[]{:S(2)}) async-start(s32[4,8,1,128]{3,1,2,0:T(8,128)} %pad_add_fusion), calls=%async_computation.1 | async-start | bytes 32768 | tf_op jit(solution)/shard_map/all_to_all | solution.py:64
  45.1 1.6 %copy-start.1 = (bf16[2,256]{1,0:T(2,128)(2,1)S(1)}, bf16[2,256]{1,0:T(2,128)(2,1)}, u32[]{:S(2)}) copy-start(bf16[2,256]{1,0:T(2,128)(2,1)} %param.16) | copy-start | bytes 3076
  45.1 1.6 %copy-start.5 = (bf16[256,256]{1,0:T(8,128)(2,1)S(1)}, bf16[256,256]{1,0:T(8,128)(2,1)}, u32[]{:S(2)}) copy-start(bf16[256,256]{1,0:T(8,128)(2,1)} %param.18) | copy-start | bytes 393220
  45.1 1.6 %copy-start.6 = (bf16[256]{0:T(256)(128)(2,1)S(1)}, bf16[256]{0:T(256)(128)(2,1)}, u32[]{:S(2)}) copy-start(bf16[256]{0:T(256)(128)(2,1)} %param.19) | copy-start | bytes 1540
  46.7 50.8 %copy-start.3 = (s32[1024,1]{0,1:T(1,128)S(1)}, s32[1024,1]{0,1:T(1,128)}, u32[]{:S(2)}) copy-start(s32[1024,1]{0,1:T(1,128)} %param.12) | copy-start | bytes 12292
  46.7 3.1 %copy-start.4 = (bf16[2,256,256]{2,1,0:T(8,128)(2,1)S(1)}, bf16[2,256,256]{2,1,0:T(8,128)(2,1)}, u32[]{:S(2)}) copy-start(bf16[2,256,256]{2,1,0:T(8,128)(2,1)} %get-tuple-element.212) | copy-start | bytes 786436 | tf_op jit(solution)/shard_map/while
  51.6 3.1 %copy-start.4 = (bf16[2,256,256]{2,1,0:T(8,128)(2,1)S(1)}, bf16[2,256,256]{2,1,0:T(8,128)(2,1)}, u32[]{:S(2)}) copy-start(bf16[2,256,256]{2,1,0:T(8,128)(2,1)} %get-tuple-element.212) | copy-start | bytes 786436 | tf_op jit(solution)/shard_map/while
  56.5 3.1 %copy-start.4 = (bf16[2,256,256]{2,1,0:T(8,128)(2,1)S(1)}, bf16[2,256,256]{2,1,0:T(8,128)(2,1)}, u32[]{:S(2)}) copy-start(bf16[2,256,256]{2,1,0:T(8,128)(2,1)} %get-tuple-element.212) | copy-start | bytes 786436 | tf_op jit(solution)/shard_map/while
  61.4 3.1 %copy-start.4 = (bf16[2,256,256]{2,1,0:T(8,128)(2,1)S(1)}, bf16[2,256,256]{2,1,0:T(8,128)(2,1)}, u32[]{:S(2)}) copy-start(bf16[2,256,256]{2,1,0:T(8,128)(2,1)} %get-tuple-element.212) | copy-start | bytes 786436 | tf_op jit(solution)/shard_map/while
  66.4 3.1 %copy-start.4 = (bf16[2,256,256]{2,1,0:T(8,128)(2,1)S(1)}, bf16[2,256,256]{2,1,0:T(8,128)(2,1)}, u32[]{:S(2)}) copy-start(bf16[2,256,256]{2,1,0:T(8,128)(2,1)} %get-tuple-element.212) | copy-start | bytes 786436 | tf_op jit(solution)/shard_map/while
  71.3 3.1 %copy-start.4 = (bf16[2,256,256]{2,1,0:T(8,128)(2,1)S(1)}, bf16[2,256,256]{2,1,0:T(8,128)(2,1)}, u32[]{:S(2)}) copy-start(bf16[2,256,256]{2,1,0:T(8,128)(2,1)} %get-tuple-element.212) | copy-start | bytes 786436 | tf_op jit(solution)/shard_map/while
  76.2 3.1 %copy-start.4 = (bf16[2,256,256]{2,1,0:T(8,128)(2,1)S(1)}, bf16[2,256,256]{2,1,0:T(8,128)(2,1)}, u32[]{:S(2)}) copy-start(bf16[2,256,256]{2,1,0:T(8,128)(2,1)} %get-tuple-element.212) | copy-start | bytes 786436 | tf_op jit(solution)/shard_map/while
  81.1 3.1 %copy-start.4 = (bf16[2,256,256]{2,1,0:T(8,128)(2,1)S(1)}, bf16[2,256,256]{2,1,0:T(8,128)(2,1)}, u32[]{:S(2)}) copy-start(bf16[2,256,256]{2,1,0:T(8,128)(2,1)} %get-tuple-element.212) | copy-start | bytes 786436 | tf_op jit(solution)/shard_map/while
  94.1 9.1 %all-to-all-start.3 = ((f32[8,5,4,128]{3,0,1,2:T(8,128)}), f32[8,5,4,128]{3,0,1,2:T(8,128)S(1)}, u32[]{:S(2)}, u32[]{:S(2)}) async-start(f32[8,5,4,128]{3,0,1,2:T(8,128)} %copy.43), calls=%async_computation.3 | async-start | bytes 163840 | tf_op jit(solution)/shard_map/all_to_all | solution.py:85
  103.8 1.2 %copy-start.2 = (f32[1,1024]{1,0:T(1,128)}, f32[1,1024]{1,0:T(1,128)S(1)}, u32[]{:S(2)}) copy-start(f32[1,1024]{1,0:T(1,128)S(1)} %get-tuple-element.108) | copy-start | bytes 12292
